TPU v7x, 32 devices: a whole 2x2x4 slice. The times are simulated.
32 devices in a mesh: dp: 8 (over z, y), tensor: 4 (over x, core).
Axes of the slice: x: 2, y: 2, z: 4, core: 2. Of those that a mesh axis runs over, the one named last changes fastest.
Arguments:
- tokens: bfloat16 [16384, 768], P(('dp', 'tensor')), may hold values from -6 to 6
- seq_lengths: int32 [8], replicated, may hold values from 1 to 2048, 10240 in all
- positions: int32 [8, 2048], P('dp'), may hold values from 0 to 2047, each once within a row
- w_query: bfloat16 [768, 768], P('dp', 'tensor'), may hold values from -0.21875 to 0.21875
- w_key: bfloat16 [768, 768], P('dp', 'tensor'), may hold values from -0.21875 to 0.21875
- w_value: bfloat16 [768, 768], P('dp', 'tensor'), may hold values from -0.21875 to 0.21875
- w_out: bfloat16 [768, 768], P('tensor', 'dp'), may hold values from -6 to 6
- w_up: bfloat16 [768, 3072], P('dp', 'tensor'), may hold values from -0.21875 to 0.21875
- w_down: bfloat16 [3072, 768], P('tensor', 'dp'), may hold values from -0.109375 to 0.109375
- b_query: bfloat16 [768], P('tensor'), may hold values from -3 to 3
- b_value: bfloat16 [768], P('tensor'), may hold values from -0.1796875 to 0.1796875
- b_out: bfloat16 [768], replicated, may hold values from -1.796875 to 1.796875
- b_up: bfloat16 [3072], P('tensor'), may hold values from -1.796875 to 1.796875
- b_down: bfloat16 [768], replicated, may hold values from -1.796875 to 1.796875
- gain_attn: bfloat16 [768], replicated, may hold values from 0.5 to 1.5
- shift_attn: bfloat16 [768], replicated, may hold values from -1.796875 to 1.796875
- gain_ffn: bfloat16 [768], replicated, may hold values from 0.5 to 1.5
- shift_ffn: bfloat16 [768], replicated, may hold values from -1.796875 to 1.796875
- out_grad: bfloat16 [16384, 768], P(('dp', 'tensor')), may hold values from -6 to 6
Outputs:
- layer_out: bfloat16 [16384, 768], P(('dp', 'tensor'))
- input_grad: bfloat16 [16384, 768], P(('dp', 'tensor'))
- grad_w_query: float32 [768, 768], P('dp', 'tensor')
- grad_w_key: float32 [768, 768], P('dp', 'tensor')
- grad_w_value: float32 [768, 768], P('dp', 'tensor')
- grad_w_out: float32 [768, 768], P('tensor', 'dp')
- grad_w_up: float32 [768, 3072], P('dp', 'tensor')
- grad_w_down: float32 [3072, 768], P('tensor', 'dp')
- grad_b_query: float32 [768], P('tensor')
- grad_b_value: float32 [768], P('tensor')
- grad_b_out: float32 [768], replicated
- grad_b_up: float32 [3072], P('tensor')
- grad_b_down: float32 [768], replicated
- grad_gain_attn: float32 [768], replicated
- grad_shift_attn: float32 [768], replicated
- grad_gain_ffn: float32 [768], replicated
- grad_shift_ffn: float32 [768], replicated
- rms: float32 [3], replicated
Inputs may be any that keep to these rules, and one draw needn't show every extreme that they name: `seq_lengths`: one length for each slot; the longest equals 2048. `positions`: each row is a permutation of 0 to 2047.
All inputs are finite; a program needn't handle non-finite values.
Results may differ from a plain program's by a relative error of at most 0.019.
Values may be sent and summed in bfloat16 or wider, within the bound.
No kernel may reach another device: no remote copies, remote signals or barrier semaphores. Data moves between devices by JAX's collectives and lax.ppermute only.
A program may use at most 128 MiB of HBM per device.

v0:
```python
import jax
import jax.numpy as jnp
from jax import lax
from jax.sharding import PartitionSpec as P

D = 768
HEAD_DIM = 64
EPSILON = 1e-12
MASKED = -1e30


def norm_rows(rows, scale_vec, shift_vec):
    average = jnp.mean(rows, axis=-1, keepdims=True)
    centred = rows - average
    variance = jnp.mean(centred * centred, axis=-1, keepdims=True)
    return centred * lax.rsqrt(variance + EPSILON) * scale_vec + shift_vec


def gelu_exact(values_in):
    return jax.nn.gelu(values_in, approximate=False)


def product(left, right):
    return jnp.dot(left, right, preferred_element_type=jnp.float32)


def product_tn(left, right):
    return lax.dot_general(
        left, right, (((0,), (0,)), ((), ())), preferred_element_type=jnp.float32
    )


def product_nt(left, right):
    return lax.dot_general(
        left, right, (((1,), (1,)), ((), ())), preferred_element_type=jnp.float32
    )


def block_scores(query_block, keys_all, key_valid, scale_value):
    scores = (
        jnp.einsum("qhd,khd->hqk", query_block, keys_all, preferred_element_type=jnp.float32)
        * scale_value
    )
    return jnp.where(key_valid[None, None, :], scores, MASKED)


def attention_forward(queries, keys_all, values_all, key_valid, block_rows):
    seq_len, heads_local, head_size = queries.shape
    scale_value = head_size ** (-0.5)

    def one_block(query_block):
        scores = block_scores(query_block, keys_all, key_valid, scale_value)
        top_score = jnp.max(scores, axis=-1, keepdims=True)
        expon = jnp.exp(scores - top_score)
        row_total = jnp.sum(expon, axis=-1, keepdims=True)
        probs = (expon / row_total).astype(jnp.bfloat16)
        attended = jnp.einsum("hqk,khd->qhd", probs, values_all, preferred_element_type=jnp.float32)
        return (attended, (top_score + jnp.log(row_total))[..., 0])

    shaped = queries.reshape(seq_len // block_rows, block_rows, heads_local, head_size)
    attended, log_total = lax.map(one_block, shaped)
    return (attended.reshape(seq_len, heads_local * head_size).astype(jnp.bfloat16), log_total)


def attention_backward(
    queries, keys_all, values_all, key_valid, log_total, grad_attended, block_rows
):
    seq_len, heads_local, head_size = queries.shape
    scale_value = head_size ** (-0.5)

    def one_block(carry, block_index):
        grad_keys, grad_values = carry
        start = block_index * block_rows
        query_block = lax.dynamic_slice_in_dim(queries, start, block_rows, 0)
        grad_block = lax.dynamic_slice_in_dim(grad_attended, start, block_rows, 0)
        scores = block_scores(query_block, keys_all, key_valid, scale_value)
        probs = jnp.exp(scores - log_total[block_index][..., None])
        grad_probs = jnp.einsum(
            "qhd,khd->hqk", grad_block, values_all, preferred_element_type=jnp.float32
        )
        row_delta = jnp.sum(probs * grad_probs, axis=-1, keepdims=True)
        grad_scores = (probs * (grad_probs - row_delta)).astype(jnp.bfloat16)
        grad_query = (
            jnp.einsum("hqk,khd->qhd", grad_scores, keys_all, preferred_element_type=jnp.float32)
            * scale_value
        )
        grad_keys = (
            grad_keys
            + jnp.einsum(
                "hqk,qhd->khd", grad_scores, query_block, preferred_element_type=jnp.float32
            )
            * scale_value
        )
        grad_values = grad_values + jnp.einsum(
            "hqk,qhd->khd",
            probs.astype(jnp.bfloat16),
            grad_block,
            preferred_element_type=jnp.float32,
        )
        return ((grad_keys, grad_values), grad_query)

    initial = (jnp.zeros(keys_all.shape, jnp.float32), jnp.zeros(values_all.shape, jnp.float32))
    (grad_keys, grad_values), grad_queries = lax.scan(
        one_block, initial, jnp.arange(seq_len // block_rows)
    )
    width_local = heads_local * head_size
    return (
        grad_queries.reshape(seq_len, width_local).astype(jnp.bfloat16),
        grad_keys.reshape(seq_len, width_local).astype(jnp.bfloat16),
        grad_values.reshape(seq_len, width_local).astype(jnp.bfloat16),
    )


def body(
    tokens,
    seq_lengths,
    positions,
    w_query,
    w_key,
    w_value,
    w_out,
    w_up,
    w_down,
    b_query,
    b_value,
    b_out,
    b_up,
    b_down,
    gain_attn,
    shift_attn,
    gain_ffn,
    shift_ffn,
    out_grad,
):
    group = lax.axis_index("dp")
    member = lax.axis_index("tensor")
    tensor_count = lax.axis_size("tensor")
    tok_rows = tokens.shape[0]
    seq_len = tok_rows * tensor_count
    block_rows = min(512, seq_len)
    length = lax.dynamic_index_in_dim(seq_lengths, group, 0, keepdims=False)
    key_valid = positions[0] < length
    row_valid = lax.dynamic_slice_in_dim(key_valid, member * tok_rows, tok_rows, 0)
    query_mat, key_mat, value_mat, out_mat, up_mat, down_mat = (
        lax.all_gather(w_query, "dp", axis=0, tiled=True),
        lax.all_gather(w_key, "dp", axis=0, tiled=True),
        lax.all_gather(w_value, "dp", axis=0, tiled=True),
        lax.all_gather(w_out, "dp", axis=1, tiled=True),
        lax.all_gather(w_up, "dp", axis=0, tiled=True),
        lax.all_gather(w_down, "dp", axis=1, tiled=True),
    )
    width_local = query_mat.shape[1]
    heads_local = width_local // HEAD_DIM
    up_local = b_up.shape[0]
    shape_heads = (seq_len, heads_local, HEAD_DIM)
    inputs_own = tokens.astype(jnp.float32)
    gathered = lax.all_gather(tokens, "tensor", axis=0, tiled=True)
    queries = (
        (product(gathered, query_mat) + b_query.astype(jnp.float32))
        .astype(jnp.bfloat16)
        .reshape(shape_heads)
    )
    keys_all = product(gathered, key_mat).astype(jnp.bfloat16).reshape(shape_heads)
    values_all = (
        (product(gathered, value_mat) + b_value.astype(jnp.float32))
        .astype(jnp.bfloat16)
        .reshape(shape_heads)
    )
    attended, log_total = attention_forward(queries, keys_all, values_all, key_valid, block_rows)
    attn_out = lax.psum_scatter(
        product(attended, out_mat), "tensor", scatter_dimension=0, tiled=True
    ) + b_out.astype(jnp.float32)
    normed, pull_one = jax.vjp(
        norm_rows,
        inputs_own + attn_out,
        gain_attn.astype(jnp.float32),
        shift_attn.astype(jnp.float32),
    )
    normed_low = normed.astype(jnp.bfloat16)
    normed_all = lax.all_gather(normed_low, "tensor", axis=0, tiled=True)
    hidden_pre = product(normed_all, up_mat) + b_up.astype(jnp.float32)
    hidden_act, pull_gelu = jax.vjp(gelu_exact, hidden_pre)
    hidden = hidden_act.astype(jnp.bfloat16)
    ffn_part = lax.psum_scatter(
        product(hidden, down_mat), "tensor", scatter_dimension=0, tiled=True
    )
    ffn_out = ffn_part + b_down.astype(jnp.float32)
    layer_out, pull_two = jax.vjp(
        norm_rows, normed + ffn_out, gain_ffn.astype(jnp.float32), shift_ffn.astype(jnp.float32)
    )
    grad_two, grad_gain_ffn, grad_shift_ffn = pull_two(out_grad.astype(jnp.float32))
    grad_ffn_low = grad_two.astype(jnp.bfloat16)
    grad_bias_down = jnp.sum(grad_ffn_low, axis=0, dtype=jnp.float32)
    grad_ffn_all = lax.all_gather(grad_ffn_low, "tensor", axis=0, tiled=True)
    grad_hidden = product_nt(grad_ffn_all, down_mat)
    grad_down = product_tn(hidden, grad_ffn_all)
    grad_pre = pull_gelu(grad_hidden)[0].astype(jnp.bfloat16)
    grad_up = product_tn(normed_all, grad_pre)
    bias_up_sum = jnp.sum(grad_pre, axis=0, dtype=jnp.float32)
    grad_bias_up = lax.dynamic_update_slice_in_dim(
        jnp.zeros((up_local * tensor_count,), jnp.float32), bias_up_sum, member * up_local, 0
    )
    grad_normed_ffn = lax.psum_scatter(
        product_nt(grad_pre, up_mat), "tensor", scatter_dimension=0, tiled=True
    )
    grad_one, grad_gain_attn, grad_shift_attn = pull_one(grad_two + grad_normed_ffn)
    grad_attn_low = grad_one.astype(jnp.bfloat16)
    grad_bias_out = jnp.sum(grad_attn_low, axis=0, dtype=jnp.float32)
    grad_attn_all = lax.all_gather(grad_attn_low, "tensor", axis=0, tiled=True)
    grad_out = product_tn(attended, grad_attn_all)
    grad_attended = product_nt(grad_attn_all, out_mat).astype(jnp.bfloat16).reshape(shape_heads)
    grad_q_low, grad_k_low, grad_v_low = attention_backward(
        queries, keys_all, values_all, key_valid, log_total, grad_attended, block_rows
    )
    grad_query = product_tn(gathered, grad_q_low)
    grad_key = product_tn(gathered, grad_k_low)
    grad_value = product_tn(gathered, grad_v_low)
    part_q = product_nt(grad_q_low, query_mat)
    part_k = product_nt(grad_k_low, key_mat)
    part_v = product_nt(grad_v_low, value_mat)
    grad_inputs = lax.psum_scatter(
        (part_q + part_k + part_v).astype(jnp.bfloat16), "tensor", scatter_dimension=0, tiled=True
    ).astype(jnp.float32)
    input_grad = (grad_one + grad_inputs).astype(jnp.bfloat16)
    summed_w = (
        lax.psum_scatter(grad_query, "dp", scatter_dimension=0, tiled=True),
        lax.psum_scatter(grad_key, "dp", scatter_dimension=0, tiled=True),
        lax.psum_scatter(grad_value, "dp", scatter_dimension=0, tiled=True),
        lax.psum_scatter(grad_out, "dp", scatter_dimension=1, tiled=True),
        lax.psum_scatter(grad_up, "dp", scatter_dimension=0, tiled=True),
        lax.psum_scatter(grad_down, "dp", scatter_dimension=1, tiled=True),
    )
    full_width = width_local * tensor_count
    bias_query_full = lax.dynamic_update_slice_in_dim(
        jnp.zeros((full_width,), jnp.float32),
        jnp.sum(grad_q_low, axis=0, dtype=jnp.float32),
        member * width_local,
        0,
    )
    bias_value_full = lax.dynamic_update_slice_in_dim(
        jnp.zeros((full_width,), jnp.float32),
        jnp.sum(grad_v_low, axis=0, dtype=jnp.float32),
        member * width_local,
        0,
    )
    row_mask = row_valid[:, None]
    squares = jnp.stack(
        [
            jnp.sum(jnp.where(row_mask, field * field, 0.0))
            for field in (inputs_own, attn_out, ffn_out)
        ]
    )
    summed = lax.psum(
        (
            bias_query_full,
            bias_value_full,
            grad_bias_out,
            grad_bias_up,
            grad_bias_down,
            grad_gain_attn,
            grad_shift_attn,
            grad_gain_ffn,
            grad_shift_ffn,
            squares,
        ),
        ("dp", "tensor"),
    )
    count = jnp.sum(seq_lengths).astype(jnp.float32) * D
    rms = jnp.sqrt(summed[9] / count)
    grad_b_query = lax.dynamic_slice_in_dim(summed[0], member * width_local, width_local, 0)
    grad_b_value = lax.dynamic_slice_in_dim(summed[1], member * width_local, width_local, 0)
    grad_b_up = lax.dynamic_slice_in_dim(summed[3], member * up_local, up_local, 0)
    return (
        layer_out.astype(jnp.bfloat16),
        input_grad,
        summed_w[0],
        summed_w[1],
        summed_w[2],
        summed_w[3],
        summed_w[4],
        summed_w[5],
        grad_b_query,
        grad_b_value,
        summed[2],
        grad_b_up,
        summed[4],
        summed[5],
        summed[6],
        summed[7],
        summed[8],
        rms,
    )


def solution(mesh):
    in_specs = (
        P(("dp", "tensor"), None),
        P(),
        P("dp", None),
        P("dp", "tensor"),
        P("dp", "tensor"),
        P("dp", "tensor"),
        P("tensor", "dp"),
        P("dp", "tensor"),
        P("tensor", "dp"),
        P("tensor"),
        P("tensor"),
        P(),
        P("tensor"),
        P(),
        P(),
        P(),
        P(),
        P(),
        P(("dp", "tensor"), None),
    )
    out_specs = (
        P(("dp", "tensor"), None),
        P(("dp", "tensor"), None),
        P("dp", "tensor"),
        P("dp", "tensor"),
        P("dp", "tensor"),
        P("tensor", "dp"),
        P("dp", "tensor"),
        P("tensor", "dp"),
        P("tensor"),
        P("tensor"),
        P(),
        P("tensor"),
        P(),
        P(),
        P(),
        P(),
        P(),
        P(),
    )
    return jax.shard_map(body, mesh=mesh, in_specs=in_specs, out_specs=out_specs, check_vma=False)
```

profile of v0, /device:TPU:0, one launch (start us, length us, event | category | flops | bytes accessed | tf_op | source)
XLA Modules:
  0.0 1126.0 jit_solution(8384975540335795945)
XLA Ops:
  12.3 32.9 %all_gather.34 = bf16[192,768]{0,1:T(8,128)(2,1)S(1)} all-gather(bf16[192,96]{0,1:T(8,128)(2,1)S(1)} %copy.49), channel_id=1, replica_groups=mesh['dp'=8,'tensor'=4] {'dp'}, dimensions={1}, use_global_device_ids=true | all-gather | bytes 331776 | tf_op jit(solution)/shard_map/all_gather | solution.py:148
  45.2 31.3 %all_gather.31 = bf16[768,192]{1,0:T(8,128)(2,1)S(1)} all-gather(bf16[96,192]{1,0:T(8,128)(2,1)} %param.26), channel_id=1, replica_groups=mesh['dp'=8,'tensor'=4] {'dp'}, dimensions={0}, use_global_device_ids=true | all-gather | bytes 331776 | tf_op jit(solution)/shard_map/all_gather | solution.py:145
  76.6 31.5 %all_gather.32 = bf16[768,192]{1,0:T(8,128)(2,1)S(1)} all-gather(bf16[96,192]{1,0:T(8,128)(2,1)} %param.27), channel_id=1, replica_groups=mesh['dp'=8,'tensor'=4] {'dp'}, dimensions={0}, use_global_device_ids=true | all-gather | bytes 331776 | tf_op jit(solution)/shard_map/all_gather | solution.py:146
  108.1 33.2 %all_gather.33 = bf16[768,192]{1,0:T(8,128)(2,1)} all-gather(bf16[96,192]{1,0:T(8,128)(2,1)} %param.28), channel_id=1, replica_groups=mesh['dp'=8,'tensor'=4] {'dp'}, dimensions={0}, use_global_device_ids=true | all-gather | bytes 331776 | tf_op jit(solution)/shard_map/all_gather | solution.py:147
  143.2 3.1 fusion.43
  147.3 3.2 convolution_convert_fusion.1
  151.8 36.4 %while.27 = (s32[]{:T(128)}, bf16[4,512,3,64]{1,3,2,0:T(8,128)(2,1)S(1)}, f32[4,3,512]{2,1,0:T(4,128)}, pred[2048]{0:T(1024)(128)(4,1)S(1)}, bf16[4,512,3,64]{1,...) while((s32[]{:T(128)}, ...), condition=%wide.region_3.4_spmd, body=%wide.region_0.3_spmd.sunk | while | flops 843053568 | bytes 39972968 | solution.py:61
  153.8 2.8 fusion.131
  156.6 3.7 fusion.132
  162.9 2.8 fusion.131
  165.7 3.7 fusion.132
  172.0 2.8 fusion.131
  174.8 3.7 fusion.132
  181.1 2.8 fusion.131
  183.9 3.7 fusion.132
  189.9 3.7 fusion.60
  195.0 58.1 %reduce-scatter.19.cloned.1.call-done = f32[512,768]{1,0:T(8,128)} async-done(((f32[2048,768]{1,0:T(8,128)}), f32[512,768]{1,0:T(8,128)}) %reduce-scatter.19.cloned.1.call-update) | async-done | bytes 1572880 | tf_op jit(solution)/shard_map/reduce_scatter | solution.py:170
  259.2 26.4 %all-gather.9.cloned.1.call-done = bf16[2048,768]{1,0:T(8,128)(2,1)} async-done(((bf16[512,768]{1,0:T(8,128)(2,1)}), bf16[2048,768]{1,0:T(8,128)(2,1)}) %all-gather.9.cloned.1.call-update) | async-done | bytes 3145744 | tf_op jit(solution)/shard_map/all_gather | solution.py:180
  285.6 18.9 %multiply_convert_fusion.1 = (bf16[2048,768]{1,0:T(8,128)(2,1)}, f32[2048,768]{1,0:T(8,128)}, f32[2048,768]{1,0:T(8,128)}) fusion(f32[768]{0:T(1024)} %convert_element_type.139, bf16[2048,768]{1,0:T(8,128)(2,1)} %all-gather.9.cloned.1.call-done, bf16[768,768]{1,0:T(8,128)(2,1)} %all-gather.11.cloned.1.call-done), kind=kOutput, calls=%fused_computation.47 | convolution fusion | flops 2519728128 | bytes 20057088 | tf_op jit(solution)/shard_map/dot_general | solution.py:24
  304.5 24.9 %all-gather.13.cloned.1.call-done = bf16[768,768]{0,1:T(8,128)(2,1)} async-done(((bf16[768,96]{0,1:T(8,128)(2,1)}), bf16[768,768]{0,1:T(8,128)(2,1)}) %all-gather.13.cloned.1.call-update) | async-done | bytes 1179664 | tf_op jit(solution)/shard_map/all_gather | solution.py:150
  329.4 7.5 fusion.61
  342.1 51.7 %reduce-scatter.21.cloned.1.call-done = f32[512,768]{1,0:T(8,128)} async-done(((f32[2048,768]{1,0:T(8,128)}), f32[512,768]{1,0:T(8,128)}) %reduce-scatter.21.cloned.1.call-update) | async-done | bytes 1572880 | tf_op jit(solution)/shard_map/reduce_scatter | solution.py:184
  393.8 4.2 fusion.49
  404.5 28.2 %all-gather.15.cloned.1.call-done = bf16[2048,768]{1,0:T(8,128)(2,1)} async-done(((bf16[512,768]{1,0:T(8,128)(2,1)}), bf16[2048,768]{1,0:T(8,128)(2,1)}) %all-gather.15.cloned.1.call-update) | async-done | bytes 3145744 | tf_op jit(solution)/shard_map/all_gather | solution.py:194
  432.7 11.1 convert_reduce_fusion
  445.4 4.6 fusion.62
  450.1 58.3 %reduce-scatter.23.cloned.1.call-done = f32[512,768]{1,0:T(8,128)} async-done(((f32[2048,768]{1,0:T(8,128)}), f32[512,768]{1,0:T(8,128)}) %reduce-scatter.23.cloned.1.call-update) | async-done | bytes 1572880 | tf_op jit(solution)/shard_map/reduce_scatter | solution.py:203
  508.4 3.3 multiply_reduce_fusion.1
  516.1 28.4 %all-gather.17.cloned.1.call-done = bf16[2048,768]{1,0:T(8,128)(2,1)} async-done(((bf16[512,768]{1,0:T(8,128)(2,1)}), bf16[2048,768]{1,0:T(8,128)(2,1)}) %all-gather.17.cloned.1.call-update) | async-done | bytes 3145744 | tf_op jit(solution)/shard_map/all_gather | solution.py:209
  544.6 4.0 convolution_convert_fusion
  549.5 119.3 %while.28 = (s32[]{:T(128)}, f32[2048,3,64]{0,2,1:T(8,128)S(1)}, f32[2048,3,64]{0,2,1:T(8,128)}, bf16[4,512,3,64]{1,3,2,0:T(8,128)(2,1)}, s32[4]{0:T(128)S(1)}, ...) while((s32[]{:T(128)}, f32[2048,3,64]{0,2,1:T(8,128)S(1)}, ...), condition=%wide.region_17.18_spmd.clone, body=%wide.region_15.17_spmd.clone.sunk | while | flops 2062514688 | bytes 129417528 | solution.py:103
  553.4 2.8 fusion.142
  556.1 4.9 fusion.144
  561.0 4.8 multiply_reduce_fusion.6
  565.9 5.0 multiply_convert_fusion.3
  570.9 5.6 fusion.145
  582.8 2.8 fusion.142
  585.5 5.5 fusion.144
  591.0 4.8 multiply_reduce_fusion.6
  595.9 5.0 multiply_convert_fusion.3
  600.9 5.6 fusion.145
  612.7 2.8 fusion.142
  615.5 5.5 fusion.144
  621.0 4.8 multiply_reduce_fusion.6
  625.9 5.0 multiply_convert_fusion.3
  630.8 5.6 fusion.145
  642.7 2.8 fusion.142
  645.5 5.5 fusion.144
  651.0 4.8 multiply_reduce_fusion.6
  655.9 5.0 multiply_convert_fusion.3
  660.8 5.6 fusion.145
  668.9 4.5 convolution_bitcast_fusion
  678.3 2.8 add_convert_fusion
  681.2 7.0 fusion.65
  688.2 6.9 fusion.66
  695.2 3.5 convolution_bitcast_fusion.3
  705.4 3.7 convolution_bitcast_fusion.1
  715.7 40.9 %all-reduce = (f32[768]{0:T(1024)S(1)}, f32[768]{0:T(1024)S(1)}, f32[768]{0:T(1024)}, f32[3072]{0:T(1024)S(1)}, f32[768]{0:T(1024)}, /*index=5*/f32[768]{0:T(102...) all-reduce(f32[768]{0:T(1024)S(1)} %dynamic_update_slice.20, ...), channel_id=1, replica_groups=mesh['dp'=8,'tensor'=4] {'dp','tensor'}, use_global_device_ids=true, to_apply=%region_26.27 | all-reduce | flops 9219 | bytes 73752 | tf_op jit(solution)/shard_map/psum | solution.py:253
  760.7 14.7 %reduce-scatter.25.cloned.1.call-done = bf16[512,768]{1,0:T(8,128)(2,1)} async-done(((bf16[2048,768]{1,0:T(8,128)(2,1)}), bf16[512,768]{1,0:T(8,128)(2,1)}) %reduce-scatter.25.cloned.1.call-update) | async-done | bytes 786448 | tf_op jit(solution)/shard_map/reduce_scatter | solution.py:221
  777.6 71.3 %reduce-scatter.27.cloned.1.call-done = f32[96,768]{1,0:T(8,128)} async-done(((f32[768,768]{1,0:T(8,128)}), f32[96,768]{1,0:T(8,128)}) %reduce-scatter.27.cloned.1.call-update) | async-done | bytes 294928 | tf_op jit(solution)/shard_map/reduce_scatter | solution.py:230
  849.0 72.3 %reduce-scatter.29.cloned.1.call-done = f32[768,96]{0,1:T(8,128)} async-done(((f32[768,768]{0,1:T(8,128)}), f32[768,96]{0,1:T(8,128)}) %reduce-scatter.29.cloned.1.call-update) | async-done | bytes 294928 | tf_op jit(solution)/shard_map/reduce_scatter | solution.py:231
  921.3 65.9 %reduce-scatter.31.cloned.1.call-done = f32[96,192]{1,0:T(8,128)} async-done(((f32[768,192]{1,0:T(8,128)}), f32[96,192]{1,0:T(8,128)}) %reduce-scatter.31.cloned.1.call-update) | async-done | bytes 73744
  987.2 65.3 %reduce-scatter.33.cloned.1.call-done = f32[96,192]{1,0:T(8,128)} async-done(((f32[768,192]{1,0:T(8,128)}), f32[96,192]{1,0:T(8,128)}) %reduce-scatter.33.cloned.1.call-update) | async-done | bytes 73744
  1052.6 65.9 %reduce-scatter.35.cloned.1.call-done = f32[96,192]{1,0:T(8,128)} async-done(((f32[768,192]{1,0:T(8,128)}), f32[96,192]{1,0:T(8,128)}) %reduce-scatter.35.cloned.1.call-update) | async-done | bytes 73744
  (201 shorter events, 85.0 us)
Async XLA Ops:
  8.0 135.2 %all-gather.7.cloned.1.call-start = ((), (), s32[]{:S(2)}) async-start(), calls=%async_computation.10 | async-start | bytes 3932160 | tf_op jit(solution)/shard_map/all_gather | solution.py:157
  8.8 244.3 %reduce-scatter.19.cloned.1.call-start = ((), (), s32[]{:S(2)}) async-start(), calls=%async_computation.11 | async-start | bytes 7864320 | tf_op jit(solution)/shard_map/reduce_scatter | solution.py:170
  76.6 70.3 %copy-start.11 = (bf16[768,192]{1,0:T(8,128)(2,1)}, bf16[768,192]{1,0:T(8,128)(2,1)S(1)}, u32[]{:S(2)}) copy-start(bf16[768,192]{1,0:T(8,128)(2,1)S(1)} %all_gather.31) | copy-start | bytes 884740
  108.0 39.3 %copy-start.8 = (bf16[768,192]{1,0:T(8,128)(2,1)}, bf16[768,192]{1,0:T(8,128)(2,1)S(1)}, u32[]{:S(2)}) copy-start(bf16[768,192]{1,0:T(8,128)(2,1)S(1)} %all_gather.32) | copy-start | bytes 884740
  146.2 0.9 copy-start.5
  147.1 3.4 copy-start.1
  147.1 3.4 copy-start.13
  189.0 0.9 copy-start.7
  193.7 0.7 copy-start.30
  193.7 0.7 copy-start.31
  193.7 0.7 copy-start.32
  193.7 65.5 %all-gather.11.cloned.1.call-start = ((), (), s32[]{:S(2)}) async-start(), calls=%async_computation.13 | async-start | bytes 1327104 | tf_op jit(solution)/shard_map/all_gather | solution.py:149
  194.3 91.3 %all-gather.9.cloned.1.call-start = ((), (), s32[]{:S(2)}) async-start(), calls=%async_computation.12 | async-start | bytes 3932160 | tf_op jit(solution)/shard_map/all_gather | solution.py:180
  194.4 60.6 %copy-start.17 = (f32[768]{0:T(1024)}, f32[768]{0:T(1024)S(1)}, u32[]{:S(2)}) copy-start(f32[768]{0:T(1024)S(1)} %convert_element_type.135) | copy-start | bytes 9220
  253.1 2.8 copy-start.15
  255.3 0.6 copy-start.18
  257.1 72.4 %all-gather.13.cloned.1.call-start = ((), (), s32[]{:S(2)}) async-start(), calls=%async_computation.14 | async-start | bytes 1327104 | tf_op jit(solution)/shard_map/all_gather | solution.py:150
  257.7 136.1 %reduce-scatter.21.cloned.1.call-start = ((), (), s32[]{:S(2)}) async-start(), calls=%async_computation.15 | async-start | bytes 7864320 | tf_op jit(solution)/shard_map/reduce_scatter | solution.py:184
  337.0 95.7 %all-gather.15.cloned.1.call-start = ((), (), s32[]{:S(2)}) async-start(), calls=%async_computation.16 | async-start | bytes 3932160 | tf_op jit(solution)/shard_map/all_gather | solution.py:194
  393.8 4.5 copy-start.10
  393.8 4.5 copy-start.16
  398.0 1.6 copy-start.26
  401.1 1.2 copy-start.4
  401.1 2.8 copy-start.19
  404.0 104.4 %reduce-scatter.23.cloned.1.call-start = ((), (), s32[]{:S(2)}) async-start(), calls=%async_computation.17 | async-start | bytes 7864320 | tf_op jit(solution)/shard_map/reduce_scatter | solution.py:203
  432.7 12.7 %copy-start.33 = (bf16[768,768]{1,0:T(8,128)(2,1)S(1)}, bf16[768,768]{1,0:T(8,128)(2,1)}, u32[]{:S(2)}) copy-start(bf16[768,768]{1,0:T(8,128)(2,1)} %all-gather.11.cloned.1.call-done) | copy-start | bytes 3538948
  443.8 1.7 copy-start.35
  450.0 94.5 %all-gather.17.cloned.1.call-start = ((), (), s32[]{:S(2)}) async-start(), calls=%async_computation.18 | async-start | bytes 3932160 | tf_op jit(solution)/shard_map/all_gather | solution.py:209
  513.0 1.2 copy-start.2
  513.0 2.8 copy-start.20
  515.9 243.2 %reduce-scatter.37.cloned.1.call-start = ((), (), s32[]{:S(2)}) async-start(), calls=%async_computation.25 | async-start | bytes 884736
  570.9 5.6 copy-start
  600.8 5.6 copy-start
  630.8 5.6 copy-start
  660.8 5.6 copy-start
  668.9 4.8 copy-start.9
  673.4 102.0 %reduce-scatter.25.cloned.1.call-start = ((), (), s32[]{:S(2)}) async-start(), calls=%async_computation.19 | async-start | bytes 3932160 | tf_op jit(solution)/shard_map/reduce_scatter | solution.py:221
  673.7 2.7 copy-start.6
  674.8 2.5 copy-start.12
  677.2 1.1 copy-start.14
  681.1 167.8 %reduce-scatter.27.cloned.1.call-start = ((), (), s32[]{:S(2)}) async-start(), calls=%async_computation.20 | async-start | bytes 2654208 | tf_op jit(solution)/shard_map/reduce_scatter | solution.py:230
  688.2 233.1 %reduce-scatter.29.cloned.1.call-start = ((), (), s32[]{:S(2)}) async-start(), calls=%async_computation.21 | async-start | bytes 2654208 | tf_op jit(solution)/shard_map/reduce_scatter | solution.py:231
  695.2 292.1 %reduce-scatter.31.cloned.1.call-start = ((), (), s32[]{:S(2)}) async-start(), calls=%async_computation.22 | async-start | bytes 884736
  701.0 351.5 %reduce-scatter.33.cloned.1.call-start = ((), (), s32[]{:S(2)}) async-start(), calls=%async_computation.23 | async-start | bytes 884736
  705.0 6.3 copy-start.34
  705.0 9.6 copy-start.29
  705.0 10.7 copy-start.22
  705.0 10.6 copy-start.23
  705.0 10.6 copy-start.24
  705.0 10.6 copy-start.25
  705.0 10.6 copy-start.27
  705.0 10.6 copy-start.28
  705.1 70.3 %copy-start.3 = (f32[512,768]{1,0:T(8,128)S(1)}, f32[512,768]{1,0:T(8,128)}, u32[]{:S(2)}) copy-start(f32[512,768]{1,0:T(8,128)} %copy-done.2) | copy-start | bytes 4718596
  705.1 70.3 %copy-start.21 = (f32[512]{0:T(512)S(1)}, f32[512]{0:T(512)}, u32[]{:S(2)}) copy-start(f32[512]{0:T(512)} %copy-done.20) | copy-start | bytes 6148
  705.1 413.3 %reduce-scatter.35.cloned.1.call-start = ((), (), s32[]{:S(2)}) async-start(), calls=%async_computation.24 | async-start | bytes 884736
Sparse Core Ops, SparseCore 0:
  10.4 31.2 all-gather.6
  193.8 59.2 reduce-scatter.18
  404.1 28.5 all-gather.14
  516.0 28.5 all-gather.16
Sparse Core Ops, SparseCore 1:
  196.6 42.3 all-gather.10
  257.2 28.4 all-gather.8
  287.9 41.5 all-gather.12
  337.0 56.7 reduce-scatter.20
  450.1 58.2 reduce-scatter.22
  673.5 62.5 reduce-scatter.36
  738.5 36.8 reduce-scatter.24
  779.7 69.2 reduce-scatter.26
  853.3 67.9 reduce-scatter.28
  925.5 61.6 reduce-scatter.30
  991.0 61.5 reduce-scatter.32
  1056.8 61.5 reduce-scatter.34
where the time goes:
time: 1140 us; the launch traced here: 1130 us
  waiting for transfers between devices  634 us (56%)
  matrix products  197 us (17%)
  blocking collectives  170 us (15%)
  other arithmetic  68.6 us (6%)
  local copies, waits for them, and re-layouts  27.8 us (2%)
  between operations  17 us (1%)
    unnamed x20, waiting for transfers between devices  199 us
    reduce_scatter x1, waiting for transfers between devices, body(): lax.psum_scatter(grad_down, 'dp', scatter_dimension=1, tiled=True)  72.3 us
    reduce_scatter x1, waiting for transfers between devices, body(): lax.psum_scatter(grad_up, 'dp', scatter_dimension=0, tiled=True)  71.3 us
    reduce_scatter x1, waiting for transfers between devices, body(): lax.psum_scatter(product_nt(grad_pre, up_mat), 'tensor', scatter_dimensio...  58.3 us
    reduce_scatter x1, waiting for transfers between devices, body(): lax.psum_scatter(product(attended, out_mat), 'tensor', scatter_dimension=...  58.1 us
    reduce_scatter x1, waiting for transfers between devices, body(): lax.psum_scatter(product(hidden, down_mat), 'tensor', scatter_dimension=0...  51.7 us
    psum x1, blocking collectives, body(): lax.psum((bias_query_full, bias_value_full, grad_bias_out, grad_bias_up,...  40.9 us
    dot_general x6, matrix products, product(): return jnp.dot(left, right, preferred_element_type=jnp.float32)  37.6 us
  transfers between devices with their start and end apart: 16, of which 13 were waited for; matrix products, arithmetic and copies ran while one was open for 7% of the time, Pallas kernels for 0%

commit v1 on v0

--- a/solution.py
+++ b/solution.py
@@ -251,19 +251,22 @@
         ]
     )
     summed = lax.psum(
-        (
-            bias_query_full,
-            bias_value_full,
-            grad_bias_out,
-            grad_bias_up,
-            grad_bias_down,
-            grad_gain_attn,
-            grad_shift_attn,
-            grad_gain_ffn,
-            grad_shift_ffn,
-            squares,
+        lax.psum(
+            (
+                bias_query_full,
+                bias_value_full,
+                grad_bias_out,
+                grad_bias_up,
+                grad_bias_down,
+                grad_gain_attn,
+                grad_shift_attn,
+                grad_gain_ffn,
+                grad_shift_ffn,
+                squares,
+            ),
+            "tensor",
         ),
-        ("dp", "tensor"),
+        "dp",
     )
     count = jnp.sum(seq_lengths).astype(jnp.float32) * D
     rms = jnp.sqrt(summed[9] / count)

time: 1140 us -> 1140 us (level)
    psum x0 -> x1, blocking collectives: none -> 38.4 us  [body(): lax.psum(lax.psum((bias_query_full, bias_value_full, grad_bias_out, grad_...]
    psum x1, blocking collectives: 40.9 us -> 10.8 us  [body(): lax.psum((bias_query_full, bias_value_full, grad_bias_out, grad_bias_up,...]
where the time goes in v1:
time: 1140 us; the launch traced here: 1130 us
  waiting for transfers between devices  625 us (55%)
  matrix products  197 us (17%)
  blocking collectives  178 us (16%)
  other arithmetic  68.6 us (6%)
  local copies, waits for them, and re-layouts  27.8 us (2%)
  between operations  17 us (1%)
    unnamed x20, waiting for transfers between devices  199 us
    reduce_scatter x1, waiting for transfers between devices, body(): lax.psum_scatter(grad_down, 'dp', scatter_dimension=1, tiled=True)  72.4 us
    reduce_scatter x1, waiting for transfers between devices, body(): lax.psum_scatter(grad_up, 'dp', scatter_dimension=0, tiled=True)  71.1 us
    reduce_scatter x1, waiting for transfers between devices, body(): lax.psum_scatter(product_nt(grad_pre, up_mat), 'tensor', scatter_dimensio...  58.3 us
    reduce_scatter x1, waiting for transfers between devices, body(): lax.psum_scatter(product(attended, out_mat), 'tensor', scatter_dimension=...  58.1 us
    reduce_scatter x1, waiting for transfers between devices, body(): lax.psum_scatter(product(hidden, down_mat), 'tensor', scatter_dimension=0...  51.7 us
    psum x1, blocking collectives, body(): lax.psum(lax.psum((bias_query_full, bias_value_full, grad_bias_out, grad_...  38.4 us
    dot_general x6, matrix products, product(): return jnp.dot(left, right, preferred_element_type=jnp.float32)  37.6 us
  transfers between devices with their start and end apart: 16, of which 13 were waited for; matrix products, arithmetic and copies ran while one was open for 7% of the time, Pallas kernels for 0%

profile of v1, /device:TPU:0, one launch (start us, length us, event | category | flops | bytes accessed | tf_op | source)
XLA Modules:
  0.0 1125.9 jit_solution(8896784130334329919)
XLA Ops:
  12.3 32.9 %all_gather.34 = bf16[192,768]{0,1:T(8,128)(2,1)S(1)} all-gather(bf16[192,96]{0,1:T(8,128)(2,1)S(1)} %copy.49), channel_id=1, replica_groups=mesh['dp'=8,'tensor'=4] {'dp'}, dimensions={1}, use_global_device_ids=true | all-gather | bytes 331776 | tf_op jit(solution)/shard_map/all_gather | solution.py:148
  45.2 31.3 %all_gather.31 = bf16[768,192]{1,0:T(8,128)(2,1)S(1)} all-gather(bf16[96,192]{1,0:T(8,128)(2,1)} %param.26), channel_id=1, replica_groups=mesh['dp'=8,'tensor'=4] {'dp'}, dimensions={0}, use_global_device_ids=true | all-gather | bytes 331776 | tf_op jit(solution)/shard_map/all_gather | solution.py:145
  76.6 31.5 %all_gather.32 = bf16[768,192]{1,0:T(8,128)(2,1)S(1)} all-gather(bf16[96,192]{1,0:T(8,128)(2,1)} %param.27), channel_id=1, replica_groups=mesh['dp'=8,'tensor'=4] {'dp'}, dimensions={0}, use_global_device_ids=true | all-gather | bytes 331776 | tf_op jit(solution)/shard_map/all_gather | solution.py:146
  108.1 33.2 %all_gather.33 = bf16[768,192]{1,0:T(8,128)(2,1)} all-gather(bf16[96,192]{1,0:T(8,128)(2,1)} %param.28), channel_id=1, replica_groups=mesh['dp'=8,'tensor'=4] {'dp'}, dimensions={0}, use_global_device_ids=true | all-gather | bytes 331776 | tf_op jit(solution)/shard_map/all_gather | solution.py:147
  143.2 3.1 fusion.43
  147.3 3.2 convolution_convert_fusion.1
  151.8 36.4 %while.27 = (s32[]{:T(128)}, bf16[4,512,3,64]{1,3,2,0:T(8,128)(2,1)S(1)}, f32[4,3,512]{2,1,0:T(4,128)}, pred[2048]{0:T(1024)(128)(4,1)S(1)}, bf16[4,512,3,64]{1,...) while((s32[]{:T(128)}, ...), condition=%wide.region_3.4_spmd, body=%wide.region_0.3_spmd.sunk | while | flops 843053568 | bytes 39972968 | solution.py:61
  153.8 2.8 fusion.131
  156.6 3.7 fusion.132
  162.9 2.8 fusion.131
  165.7 3.7 fusion.132
  172.0 2.8 fusion.131
  174.8 3.7 fusion.132
  181.1 2.8 fusion.131
  183.9 3.7 fusion.132
  189.9 3.7 fusion.60
  195.0 58.1 %reduce-scatter.19.cloned.1.call-done = f32[512,768]{1,0:T(8,128)} async-done(((f32[2048,768]{1,0:T(8,128)}), f32[512,768]{1,0:T(8,128)}) %reduce-scatter.19.cloned.1.call-update) | async-done | bytes 1572880 | tf_op jit(solution)/shard_map/reduce_scatter | solution.py:170
  259.2 26.4 %all-gather.9.cloned.1.call-done = bf16[2048,768]{1,0:T(8,128)(2,1)} async-done(((bf16[512,768]{1,0:T(8,128)(2,1)}), bf16[2048,768]{1,0:T(8,128)(2,1)}) %all-gather.9.cloned.1.call-update) | async-done | bytes 3145744 | tf_op jit(solution)/shard_map/all_gather | solution.py:180
  285.6 18.9 %multiply_convert_fusion.1 = (bf16[2048,768]{1,0:T(8,128)(2,1)}, f32[2048,768]{1,0:T(8,128)}, f32[2048,768]{1,0:T(8,128)}) fusion(f32[768]{0:T(1024)} %convert_element_type.139, bf16[2048,768]{1,0:T(8,128)(2,1)} %all-gather.9.cloned.1.call-done, bf16[768,768]{1,0:T(8,128)(2,1)} %all-gather.11.cloned.1.call-done), kind=kOutput, calls=%fused_computation.47 | convolution fusion | flops 2519728128 | bytes 20057088 | tf_op jit(solution)/shard_map/dot_general | solution.py:24
  304.5 24.9 %all-gather.13.cloned.1.call-done = bf16[768,768]{0,1:T(8,128)(2,1)} async-done(((bf16[768,96]{0,1:T(8,128)(2,1)}), bf16[768,768]{0,1:T(8,128)(2,1)}) %all-gather.13.cloned.1.call-update) | async-done | bytes 1179664 | tf_op jit(solution)/shard_map/all_gather | solution.py:150
  329.4 7.5 fusion.61
  342.1 51.7 %reduce-scatter.21.cloned.1.call-done = f32[512,768]{1,0:T(8,128)} async-done(((f32[2048,768]{1,0:T(8,128)}), f32[512,768]{1,0:T(8,128)}) %reduce-scatter.21.cloned.1.call-update) | async-done | bytes 1572880 | tf_op jit(solution)/shard_map/reduce_scatter | solution.py:184
  393.8 4.2 fusion.49
  404.5 28.2 %all-gather.15.cloned.1.call-done = bf16[2048,768]{1,0:T(8,128)(2,1)} async-done(((bf16[512,768]{1,0:T(8,128)(2,1)}), bf16[2048,768]{1,0:T(8,128)(2,1)}) %all-gather.15.cloned.1.call-update) | async-done | bytes 3145744 | tf_op jit(solution)/shard_map/all_gather | solution.py:194
  432.7 11.1 convert_reduce_fusion
  445.4 4.6 fusion.62
  450.1 58.3 %reduce-scatter.23.cloned.1.call-done = f32[512,768]{1,0:T(8,128)} async-done(((f32[2048,768]{1,0:T(8,128)}), f32[512,768]{1,0:T(8,128)}) %reduce-scatter.23.cloned.1.call-update) | async-done | bytes 1572880 | tf_op jit(solution)/shard_map/reduce_scatter | solution.py:203
  508.4 3.3 multiply_reduce_fusion.1
  516.1 28.4 %all-gather.17.cloned.1.call-done = bf16[2048,768]{1,0:T(8,128)(2,1)} async-done(((bf16[512,768]{1,0:T(8,128)(2,1)}), bf16[2048,768]{1,0:T(8,128)(2,1)}) %all-gather.17.cloned.1.call-update) | async-done | bytes 3145744 | tf_op jit(solution)/shard_map/all_gather | solution.py:209
  544.6 4.0 convolution_convert_fusion
  549.5 119.3 %while.28 = (s32[]{:T(128)}, f32[2048,3,64]{0,2,1:T(8,128)S(1)}, f32[2048,3,64]{0,2,1:T(8,128)}, bf16[4,512,3,64]{1,3,2,0:T(8,128)(2,1)}, s32[4]{0:T(128)S(1)}, ...) while((s32[]{:T(128)}, f32[2048,3,64]{0,2,1:T(8,128)S(1)}, ...), condition=%wide.region_17.18_spmd.clone, body=%wide.region_15.17_spmd.clone.sunk | while | flops 2062514688 | bytes 129417528 | solution.py:103
  553.4 2.8 fusion.142
  556.1 4.9 fusion.144
  561.0 4.8 multiply_reduce_fusion.6
  565.9 5.0 multiply_convert_fusion.3
  570.9 5.6 fusion.145
  582.8 2.8 fusion.142
  585.5 5.5 fusion.144
  591.0 4.8 multiply_reduce_fusion.6
  595.9 5.0 multiply_convert_fusion.3
  600.9 5.6 fusion.145
  612.7 2.8 fusion.142
  615.5 5.5 fusion.144
  621.0 4.8 multiply_reduce_fusion.6
  625.9 5.0 multiply_convert_fusion.3
  630.8 5.6 fusion.145
  645.5 5.5 fusion.144
  651.0 4.8 multiply_reduce_fusion.6
  655.9 5.0 multiply_convert_fusion.3
  660.8 5.6 fusion.145
  668.9 4.5 convolution_bitcast_fusion
  678.3 2.8 add_convert_fusion
  681.2 7.0 fusion.65
  688.2 6.9 fusion.66
  695.2 3.5 convolution_bitcast_fusion.3
  705.4 3.7 convolution_bitcast_fusion.1
  715.7 10.8 all-reduce.1
  726.5 38.4 %all-reduce = (f32[768]{0:T(1024)S(1)}, f32[768]{0:T(1024)S(1)}, f32[768]{0:T(1024)}, f32[3072]{0:T(1024)S(1)}, f32[768]{0:T(1024)}, /*index=5*/f32[768]{0:T(102...) all-reduce(f32[768]{0:T(1024)S(1)} %get-tuple-element.286, ...), channel_id=1, replica_groups=mesh['dp'=8,'tensor'=4] {'dp'}, use_global_device_ids=true, to_apply=%region_27.28 | all-reduce | flops 9219 | bytes 73752 | tf_op jit(solution)/shard_map/psum | solution.py:253
  769.0 6.5 reduce-scatter.25.cloned.1.call-done
  777.8 71.1 %reduce-scatter.27.cloned.1.call-done = f32[96,768]{1,0:T(8,128)} async-done(((f32[768,768]{1,0:T(8,128)}), f32[96,768]{1,0:T(8,128)}) %reduce-scatter.27.cloned.1.call-update) | async-done | bytes 294928 | tf_op jit(solution)/shard_map/reduce_scatter | solution.py:230
  848.8 72.4 %reduce-scatter.29.cloned.1.call-done = f32[768,96]{0,1:T(8,128)} async-done(((f32[768,768]{0,1:T(8,128)}), f32[768,96]{0,1:T(8,128)}) %reduce-scatter.29.cloned.1.call-update) | async-done | bytes 294928 | tf_op jit(solution)/shard_map/reduce_scatter | solution.py:231
  921.2 65.9 %reduce-scatter.31.cloned.1.call-done = f32[96,192]{1,0:T(8,128)} async-done(((f32[768,192]{1,0:T(8,128)}), f32[96,192]{1,0:T(8,128)}) %reduce-scatter.31.cloned.1.call-update) | async-done | bytes 73744
  987.1 65.4 %reduce-scatter.33.cloned.1.call-done = f32[96,192]{1,0:T(8,128)} async-done(((f32[768,192]{1,0:T(8,128)}), f32[96,192]{1,0:T(8,128)}) %reduce-scatter.33.cloned.1.call-update) | async-done | bytes 73744
  1052.5 65.8 %reduce-scatter.35.cloned.1.call-done = f32[96,192]{1,0:T(8,128)} async-done(((f32[768,192]{1,0:T(8,128)}), f32[96,192]{1,0:T(8,128)}) %reduce-scatter.35.cloned.1.call-update) | async-done | bytes 73744
  (202 shorter events, 87.7 us)
Async XLA Ops:
  8.0 135.2 %all-gather.7.cloned.1.call-start = ((), (), s32[]{:S(2)}) async-start(), calls=%async_computation.10 | async-start | bytes 3932160 | tf_op jit(solution)/shard_map/all_gather | solution.py:157
  8.8 244.3 %reduce-scatter.19.cloned.1.call-start = ((), (), s32[]{:S(2)}) async-start(), calls=%async_computation.11 | async-start | bytes 7864320 | tf_op jit(solution)/shard_map/reduce_scatter | solution.py:170
  76.6 70.3 %copy-start.11 = (bf16[768,192]{1,0:T(8,128)(2,1)}, bf16[768,192]{1,0:T(8,128)(2,1)S(1)}, u32[]{:S(2)}) copy-start(bf16[768,192]{1,0:T(8,128)(2,1)S(1)} %all_gather.31) | copy-start | bytes 884740
  108.0 39.3 %copy-start.8 = (bf16[768,192]{1,0:T(8,128)(2,1)}, bf16[768,192]{1,0:T(8,128)(2,1)S(1)}, u32[]{:S(2)}) copy-start(bf16[768,192]{1,0:T(8,128)(2,1)S(1)} %all_gather.32) | copy-start | bytes 884740
  146.2 0.9 copy-start.5
  147.1 3.4 copy-start.1
  147.1 3.4 copy-start.13
  189.0 0.9 copy-start.7
  193.7 0.7 copy-start.30
  193.7 0.7 copy-start.31
  193.7 0.7 copy-start.32
  193.7 65.5 %all-gather.11.cloned.1.call-start = ((), (), s32[]{:S(2)}) async-start(), calls=%async_computation.13 | async-start | bytes 1327104 | tf_op jit(solution)/shard_map/all_gather | solution.py:149
  194.3 91.3 %all-gather.9.cloned.1.call-start = ((), (), s32[]{:S(2)}) async-start(), calls=%async_computation.12 | async-start | bytes 3932160 | tf_op jit(solution)/shard_map/all_gather | solution.py:180
  194.4 60.6 %copy-start.17 = (f32[768]{0:T(1024)}, f32[768]{0:T(1024)S(1)}, u32[]{:S(2)}) copy-start(f32[768]{0:T(1024)S(1)} %convert_element_type.135) | copy-start | bytes 9220
  253.1 2.8 copy-start.15
  255.3 0.6 copy-start.18
  257.1 72.4 %all-gather.13.cloned.1.call-start = ((), (), s32[]{:S(2)}) async-start(), calls=%async_computation.14 | async-start | bytes 1327104 | tf_op jit(solution)/shard_map/all_gather | solution.py:150
  257.7 136.1 %reduce-scatter.21.cloned.1.call-start = ((), (), s32[]{:S(2)}) async-start(), calls=%async_computation.15 | async-start | bytes 7864320 | tf_op jit(solution)/shard_map/reduce_scatter | solution.py:184
  337.0 95.7 %all-gather.15.cloned.1.call-start = ((), (), s32[]{:S(2)}) async-start(), calls=%async_computation.16 | async-start | bytes 3932160 | tf_op jit(solution)/shard_map/all_gather | solution.py:194
  393.8 4.5 copy-start.10
  393.8 4.5 copy-start.16
  398.0 1.6 copy-start.26
  401.1 1.2 copy-start.4
  401.1 2.8 copy-start.19
  404.0 104.4 %reduce-scatter.23.cloned.1.call-start = ((), (), s32[]{:S(2)}) async-start(), calls=%async_computation.17 | async-start | bytes 7864320 | tf_op jit(solution)/shard_map/reduce_scatter | solution.py:203
  432.7 12.7 %copy-start.33 = (bf16[768,768]{1,0:T(8,128)(2,1)S(1)}, bf16[768,768]{1,0:T(8,128)(2,1)}, u32[]{:S(2)}) copy-start(bf16[768,768]{1,0:T(8,128)(2,1)} %all-gather.11.cloned.1.call-done) | copy-start | bytes 3538948
  443.8 1.7 copy-start.35
  450.0 94.5 %all-gather.17.cloned.1.call-start = ((), (), s32[]{:S(2)}) async-start(), calls=%async_computation.18 | async-start | bytes 3932160 | tf_op jit(solution)/shard_map/all_gather | solution.py:209
  513.0 1.2 copy-start.2
  513.0 2.8 copy-start.20
  515.9 251.5 %reduce-scatter.37.cloned.1.call-start = ((), (), s32[]{:S(2)}) async-start(), calls=%async_computation.25 | async-start | bytes 884736
  570.9 5.6 copy-start
  600.8 5.6 copy-start
  630.8 5.6 copy-start
  660.8 5.6 copy-start
  668.9 4.8 copy-start.9
  673.4 102.1 %reduce-scatter.25.cloned.1.call-start = ((), (), s32[]{:S(2)}) async-start(), calls=%async_computation.19 | async-start | bytes 3932160 | tf_op jit(solution)/shard_map/reduce_scatter | solution.py:221
  673.7 2.7 copy-start.6
  674.8 2.5 copy-start.12
  677.2 1.1 copy-start.14
  681.1 167.7 %reduce-scatter.27.cloned.1.call-start = ((), (), s32[]{:S(2)}) async-start(), calls=%async_computation.20 | async-start | bytes 2654208 | tf_op jit(solution)/shard_map/reduce_scatter | solution.py:230
  688.2 233.0 %reduce-scatter.29.cloned.1.call-start = ((), (), s32[]{:S(2)}) async-start(), calls=%async_computation.21 | async-start | bytes 2654208 | tf_op jit(solution)/shard_map/reduce_scatter | solution.py:231
  695.2 291.9 %reduce-scatter.31.cloned.1.call-start = ((), (), s32[]{:S(2)}) async-start(), calls=%async_computation.22 | async-start | bytes 884736
  701.0 351.5 %reduce-scatter.33.cloned.1.call-start = ((), (), s32[]{:S(2)}) async-start(), calls=%async_computation.23 | async-start | bytes 884736
  705.0 6.3 copy-start.34
  705.0 9.6 copy-start.29
  705.0 10.7 copy-start.22
  705.0 10.6 copy-start.23
  705.0 10.6 copy-start.24
  705.0 10.6 copy-start.25
  705.0 10.6 copy-start.27
  705.0 10.6 copy-start.28
  705.1 70.4 %copy-start.3 = (f32[512,768]{1,0:T(8,128)S(1)}, f32[512,768]{1,0:T(8,128)}, u32[]{:S(2)}) copy-start(f32[512,768]{1,0:T(8,128)} %copy-done.2) | copy-start | bytes 4718596
  705.1 70.4 %copy-start.21 = (f32[512]{0:T(512)S(1)}, f32[512]{0:T(512)}, u32[]{:S(2)}) copy-start(f32[512]{0:T(512)} %copy-done.20) | copy-start | bytes 6148
  705.1 413.3 %reduce-scatter.35.cloned.1.call-start = ((), (), s32[]{:S(2)}) async-start(), calls=%async_computation.24 | async-start | bytes 884736
Sparse Core Ops, SparseCore 0:
  10.4 31.2 all-gather.6
  193.8 59.2 reduce-scatter.18
  404.1 28.5 all-gather.14
  516.0 28.5 all-gather.16
Sparse Core Ops, SparseCore 1:
  196.6 42.3 all-gather.10
  257.2 28.4 all-gather.8
  287.9 41.5 all-gather.12
  337.0 56.7 reduce-scatter.20
  450.1 58.2 reduce-scatter.22
  673.5 62.5 reduce-scatter.36
  738.5 36.9 reduce-scatter.24
  779.8 68.9 reduce-scatter.26
  853.2 68.0 reduce-scatter.28
  925.4 61.6 reduce-scatter.30
  990.9 61.6 reduce-scatter.32
  1056.7 61.5 reduce-scatter.34
